TPU v7x, 32 devices: a whole 2x2x4 slice. The times are simulated.
32 devices in a mesh: segment: 4 (over y, core), vol: 8 (over z, x).
Axes of the slice: x: 2, y: 2, z: 4, core: 2. Of those that a mesh axis runs over, the one named last changes fastest.
Arguments:
- cotangent: bfloat16 [64, 32, 256], P(None, 'vol'), may hold values from -6 to 6
- labels: int32 [32, 256], P('vol'), may hold values from 0 to 2
- class_weight: float32 [3], replicated, may hold values from 0.25 to 2
- inputs: bfloat16 [4, 64, 32, 256], P('segment', None, 'vol'), may hold values from -6 to 6
- fine_pre: bfloat16 [4, 64, 32, 256], P('segment', None, 'vol'), may hold values from -6 to 6
- pooled: bfloat16 [4, 64, 8, 128], P('segment', None, 'vol'), may hold values from -6 to 6
- coarse_pre: bfloat16 [4, 64, 8, 128], P('segment', None, 'vol'), may hold values from -6 to 6
- fine_filters: bfloat16 [4, 27, 64, 64], P('segment'), may hold values from -0.15625 to 0.15625
- coarse_filters: bfloat16 [4, 27, 64, 64], P('segment'), may hold values from -0.15625 to 0.15625
Outputs:
- input_grads: bfloat16 [4, 64, 32, 256], P('segment', None, 'vol')
- fine_filter_grads: float32 [4, 27, 64, 64], P('segment')
- coarse_filter_grads: float32 [4, 27, 64, 64], P('segment')
Inputs may be any that keep to these rules, and one draw needn't show every extreme that they name: `labels`: 0 is background, 1 fault, 2 horizon.
All inputs are finite; a program needn't handle non-finite values.
Results may differ from a plain program's by a relative error of at most 0.02.
Values may be sent and summed in bfloat16 or wider, within the bound.
A program may use at most 64 MiB of HBM per device.

v0:
```python
import math
import jax
import jax.numpy as jnp
from jax import lax
from jax.sharding import PartitionSpec as P

XL = 16


def shortened(array):
    return jax.tree.map(lambda a: a.astype(jnp.bfloat16) if a.dtype == jnp.float32 else a, array)


def padded_2(block, sides, width):
    for axis, dim in sides:
        count = lax.axis_size(axis)
        forward = [(i, i + 1) for i in range(count - 1)]
        backward = [(target, source) for source, target in forward]
        low = lax.ppermute(
            lax.slice_in_dim(block, block.shape[dim] - width, None, axis=dim), axis, forward
        )
        high = lax.ppermute(lax.slice_in_dim(block, 0, width, axis=dim), axis, backward)
        block = jnp.concatenate([low, block, high], axis=dim)
    return block


def from_behind(array, axis, by):
    devices = lax.axis_size(axis)
    pairs = [(i, i + by) for i in range(devices) if 0 <= i + by < devices]
    return lax.ppermute(array, axis, pairs)


def plane_shift(volume, columns, row_step, col_step):
    length = volume.shape[-1]
    offset = row_step * columns + col_step
    margin = columns + 1
    widths = [(0, 0)] * (volume.ndim - 1) + [(margin, margin)]
    padded = jnp.pad(volume, widths)
    shifted = lax.slice_in_dim(
        padded, margin - offset, margin - offset + length, axis=volume.ndim - 1
    )
    column = lax.broadcasted_iota(jnp.int32, (length,), 0) % columns
    inside = (column >= col_step) & (column < columns + col_step)
    return jnp.where(inside, shifted, jnp.zeros_like(shifted))


def tap_pieces(padded, columns):
    slab_count = padded.shape[1] - 2
    pieces = {}
    for middle_tap in range(3):
        for inner_tap in range(3):
            moved_plane = plane_shift(padded, columns, middle_tap - 1, inner_tap - 1)
            for outer_tap in range(3):
                pieces[outer_tap, middle_tap, inner_tap] = lax.slice_in_dim(
                    moved_plane, 2 - outer_tap, 2 - outer_tap + slab_count, axis=1
                )
    return pieces


def kernel_view(weights):
    kernel = weights.reshape(3, 3, 3, weights.shape[1], weights.shape[2])
    return kernel


def back_sum(pieces, weights):
    kernel = kernel_view(weights)
    summed = None
    for tap_key in sorted(pieces):
        term = jnp.einsum(
            "io,orp->irp", kernel[tap_key], pieces[tap_key], preferred_element_type=jnp.float32
        )
        summed = term if summed is None else summed + term
    return summed


def filter_grid(pieces, saved_local):
    outer_list = []
    for outer_tap in range(3):
        middle_list = []
        for middle_tap in range(3):
            inner_list = []
            for inner_tap in range(3):
                inner_list.append(
                    jnp.einsum(
                        "irp,orp->io",
                        saved_local,
                        pieces[outer_tap, middle_tap, inner_tap],
                        preferred_element_type=jnp.float32,
                    )
                )
            middle_list.append(jnp.stack(inner_list))
        outer_list.append(jnp.stack(middle_list))
    tap_grid = jnp.stack(outer_list)
    return tap_grid.reshape(27, tap_grid.shape[3], tap_grid.shape[4])


def edge_rims(payload):
    return padded_2(shortened(payload), (("vol", 1),), 1).astype(payload.dtype)


def to_depth(payload, half_cols):
    channels = payload.shape[0]
    full_depth = payload.shape[2] // half_cols
    shaped = payload.reshape(channels, full_depth, 1, half_cols)
    moved = lax.all_to_all(
        shortened(shaped), "vol", split_axis=1, concat_axis=2, tiled=True
    ).astype(shaped.dtype)
    return moved.reshape(channels, moved.shape[1], moved.shape[2] * half_cols)


def pool_sum(grad_wide, half_depth, half_rows, half_cols):
    channels = grad_wide.shape[0]
    blocks = grad_wide.reshape(channels, half_depth, 2, half_rows, 2, half_cols, 2)
    return blocks.sum(axis=(2, 4, 6)).reshape(channels, half_depth, half_rows * half_cols)


def spread_up(coarse_back, half_depth, half_rows, half_cols):
    channels = coarse_back.shape[0]
    widened = coarse_back.astype(jnp.float32).reshape(
        channels, half_depth, 1, half_rows, 1, half_cols, 1
    )
    widened = jnp.broadcast_to(widened, (channels, half_depth, 2, half_rows, 2, half_cols, 2))
    return widened.reshape(channels, 2 * half_depth, 8 * half_rows * half_cols // 2)


def on_device(
    cotangent,
    labels,
    class_weight,
    inputs,
    fine_pre,
    pooled,
    coarse_pre,
    fine_filters,
    coarse_filters,
):
    segments = lax.axis_size("segment")
    vol_count = lax.axis_size("vol")
    position = lax.axis_index("segment")
    channels = inputs.shape[1]
    depth_len = inputs.shape[2]
    plane_len = inputs.shape[3]
    inline_len = plane_len // XL
    half_cols = XL // 2
    half_depth = depth_len // 2
    half_inline = inline_len // 2
    cell_weight = jnp.zeros(labels.shape, jnp.float32)
    for class_index in range(class_weight.shape[0]):
        cell_weight = cell_weight + jnp.where(labels == class_index, class_weight[class_index], 0.0)
    seed_grad = (cotangent.astype(jnp.float32) * cell_weight[None]).astype(jnp.bfloat16)
    coarse_pair = jnp.concatenate([pooled[0], coarse_pre[0]], axis=0)
    stacked = to_depth(coarse_pair, half_cols)
    coarse_saved = stacked[:channels]
    coarse_mask = stacked[channels:] > 0
    saved_input = inputs[0]
    fine_mask = fine_pre[0] > 0
    fine_kernel = fine_filters[0]
    coarse_kernel = coarse_filters[0]
    incoming = jnp.where(position == segments - 1, seed_grad, jnp.zeros_like(seed_grad))

    def advance(turn_index, carry):
        gradient, grad_keep, fine_keep, coarse_keep = carry
        grad_wide = gradient.astype(jnp.float32)
        coarse_grad = pool_sum(grad_wide, half_depth, half_inline, half_cols).astype(jnp.bfloat16)
        coarse_gz = jnp.where(coarse_mask, coarse_grad, jnp.zeros_like(coarse_grad))
        coarse_pad = edge_rims(coarse_gz)
        coarse_back = back_sum(tap_pieces(coarse_pad, half_cols), coarse_kernel).astype(
            jnp.bfloat16
        )
        fine_grad = grad_wide + 0.125 * spread_up(coarse_back, half_depth, half_inline, half_cols)
        fine_gz = jnp.where(fine_mask, fine_grad, 0.0).astype(jnp.bfloat16)
        fine_pad = edge_rims(fine_gz)
        out_grad = (grad_wide + back_sum(tap_pieces(fine_pad, XL), fine_kernel)).astype(
            jnp.bfloat16
        )
        active = turn_index == segments - 1 - position
        grad_keep = jnp.where(active, out_grad, grad_keep)
        fine_keep = jnp.where(active, fine_pad, fine_keep)
        coarse_keep = jnp.where(active, coarse_pad, coarse_keep)
        passed = from_behind(out_grad, "segment", -1)
        return (passed, grad_keep, fine_keep, coarse_keep)

    start = (
        incoming,
        jnp.zeros(saved_input.shape, jnp.bfloat16),
        jnp.zeros((channels, depth_len + 2, plane_len), jnp.bfloat16),
        jnp.zeros((channels, coarse_saved.shape[1] + 2, coarse_saved.shape[2]), jnp.bfloat16),
    )
    finished = lax.fori_loop(0, segments, advance, start)
    grad_result = finished[1]
    fine_local = filter_grid(tap_pieces(finished[2], XL), saved_input)
    coarse_local = filter_grid(tap_pieces(finished[3], half_cols), coarse_saved)
    fine_total, coarse_total = (
        lax.psum(fine_local.astype(jnp.bfloat16), "vol").astype(jnp.float32),
        lax.psum(coarse_local.astype(jnp.bfloat16), "vol").astype(jnp.float32),
    )
    fine_cells = depth_len * vol_count * plane_len
    fine_total = fine_total * (1.0 / math.sqrt(fine_cells))
    coarse_total = coarse_total * (1.0 / math.sqrt(fine_cells // 8))
    return (grad_result[None], fine_total[None], coarse_total[None])


def solution(mesh):
    return jax.shard_map(
        on_device,
        mesh=mesh,
        in_specs=(
            P(None, "vol", None),
            P("vol", None),
            P(),
            P("segment", None, "vol", None),
            P("segment", None, "vol", None),
            P("segment", None, "vol", None),
            P("segment", None, "vol", None),
            P("segment", None, None, None),
            P("segment", None, None, None),
        ),
        out_specs=(
            P("segment", None, "vol", None),
            P("segment", None, None, None),
            P("segment", None, None, None),
        ),
        check_vma=False,
    )
```

profile of v0, /device:TPU:0, one launch (start us, length us, event | category | flops | bytes accessed | tf_op | source)
XLA Modules:
  0.0 262.4 jit_solution(14999166391219055556)
XLA Ops:
  7.2 0.9 copy.181
  8.3 0.7 maximum_bitcast_fusion.24
  9.0 7.3 %all-to-all-start = ((bf16[128,16,1,8]{0,3,2,1:T(8,128)(2,1)}), bf16[128,16,1,8]{0,3,2,1:T(8,128)(2,1)S(1)}, u32[]{:S(2)}, u32[]{:S(2)}) async-start(bf16[128,16,1,8]{0,3,2,1:T(8,128)(2,1)} %maximum_bitcast_fusion.24), calls=%async_computation | async-start | bytes 65536 | tf_op jit(solution)/shard_map/all_to_all | solution.py:105
  16.4 1.4 fusion.382
  17.9 2.7 %select_add_fusion = f32[4,256]{1,0:T(4,128)S(1)} fusion(s32[4,256]{1,0:T(4,128)} %param.12, f32[]{:T(128)} %bitcast.2, f32[]{:T(128)} %bitcast.1, f32[]{:T(128)} %bitcast), kind=kLoop, calls=%fused_computation.494 | loop fusion | flops 8192 | bytes 8204 | tf_op jit(solution)/shard_map/add | solution.py:149
  20.6 2.4 all-to-all-done
  23.0 130.6 %while.23 = (s32[]{:T(128)}, bf16[64,4,256]{2,0,1:T(8,128)(2,1)S(1)}, bf16[64,4,256]{2,0,1:T(8,128)(2,1)S(1)}, bf16[64,6,256]{2,0,1:T(8,128)(2,1)S(1)}, bf16[64,...) while((s32[]{:T(128)}, ...), condition=%wide.region_2.3_spmd.clone, body=%wide.region_0.2_spmd.clone.sunk | while | flops 259488704 | bytes 29859644 | solution.py:189
  23.2 0.4 reduce_sum.19
  23.6 1.3 collective-permute-start
  24.9 4.5 %collective-permute-start.1 = (bf16[64,1,64]{0,2,1:T(8,128)(2,1)S(1)}, bf16[64,1,64]{0,2,1:T(8,128)(2,1)S(1)}, u32[]{:S(2)}, u32[]{:S(2)}) collective-permute-start(bf16[64,1,64]{0,2,1:T(8,128)(2,1)S(1)} %get-tuple-element.480), channel_id=1, source_target_pairs={{0,1},{1,2},{2,3},{3,4},{4,5},{5,6},{6,7},{8,9},{9,10},{10,11},{11... | collective-permute-start | bytes 24584 | tf_op jit(solution)/shard_map/while/body/eval_jaxpr/ppermute | solution.py:19
  29.5 1.4 collective-permute-done.1
  36.6 1.3 collective-permute-start.2
  37.9 4.8 %collective-permute-start.3 = (bf16[64,1,256]{2,0,1:T(8,128)(2,1)S(1)}, bf16[64,1,256]{2,0,1:T(8,128)(2,1)S(1)}, u32[]{:S(2)}, u32[]{:S(2)}) collective-permute-start(bf16[64,1,256]{2,0,1:T(8,128)(2,1)S(1)} %get-tuple-element.483), channel_id=1, source_target_pairs={{0,1},{1,2},{2,3},{3,4},{4,5},{5,6},{6,7},{8,9},{9,10},{10,11},{11... | collective-permute-start | bytes 98312 | tf_op jit(solution)/shard_map/while/body/eval_jaxpr/ppermute | solution.py:19
  42.8 1.6 collective-permute-done.3
  44.5 0.6 fusion.555
  45.1 0.4 copy-done.2
  50.2 1.3 collective-permute-start.4
  51.5 1.9 collective-permute-done.4
  53.5 0.4 reduce_sum.19
  54.0 1.3 collective-permute-start
  55.3 5.4 %collective-permute-start.1 = (bf16[64,1,64]{0,2,1:T(8,128)(2,1)S(1)}, bf16[64,1,64]{0,2,1:T(8,128)(2,1)S(1)}, u32[]{:S(2)}, u32[]{:S(2)}) collective-permute-start(bf16[64,1,64]{0,2,1:T(8,128)(2,1)S(1)} %get-tuple-element.480), channel_id=1, source_target_pairs={{0,1},{1,2},{2,3},{3,4},{4,5},{5,6},{6,7},{8,9},{9,10},{10,11},{11... | collective-permute-start | bytes 24584 | tf_op jit(solution)/shard_map/while/body/eval_jaxpr/ppermute | solution.py:19
  60.8 1.4 collective-permute-done.1
  67.9 1.3 collective-permute-start.2
  69.2 5.8 %collective-permute-start.3 = (bf16[64,1,256]{2,0,1:T(8,128)(2,1)S(1)}, bf16[64,1,256]{2,0,1:T(8,128)(2,1)S(1)}, u32[]{:S(2)}, u32[]{:S(2)}) collective-permute-start(bf16[64,1,256]{2,0,1:T(8,128)(2,1)S(1)} %get-tuple-element.483), channel_id=1, source_target_pairs={{0,1},{1,2},{2,3},{3,4},{4,5},{5,6},{6,7},{8,9},{9,10},{10,11},{11... | collective-permute-start | bytes 98312 | tf_op jit(solution)/shard_map/while/body/eval_jaxpr/ppermute | solution.py:19
  75.0 1.6 collective-permute-done.3
  76.7 0.6 fusion.555
  77.3 0.4 copy-done.2
  82.3 1.3 collective-permute-start.4
  83.6 2.7 %collective-permute-done.4 = bf16[64,4,256]{2,0,1:T(8,128)(2,1)S(1)} collective-permute-done((bf16[64,4,256]{2,0,1:T(8,128)(2,1)S(1)}, bf16[64,4,256]{2,0,1:T(8,128)(2,1)S(1)}, u32[]{:S(2)}, u32[]{:S(2)}) %collective-permute-start.4) | collective-permute-done | bytes 131104 | tf_op jit(solution)/shard_map/while/body/eval_jaxpr/ppermute | solution.py:30
  86.5 0.4 reduce_sum.19
  86.9 1.3 collective-permute-start
  88.2 5.4 %collective-permute-start.1 = (bf16[64,1,64]{0,2,1:T(8,128)(2,1)S(1)}, bf16[64,1,64]{0,2,1:T(8,128)(2,1)S(1)}, u32[]{:S(2)}, u32[]{:S(2)}) collective-permute-start(bf16[64,1,64]{0,2,1:T(8,128)(2,1)S(1)} %get-tuple-element.480), channel_id=1, source_target_pairs={{0,1},{1,2},{2,3},{3,4},{4,5},{5,6},{6,7},{8,9},{9,10},{10,11},{11... | collective-permute-start | bytes 24584 | tf_op jit(solution)/shard_map/while/body/eval_jaxpr/ppermute | solution.py:19
  93.7 1.4 collective-permute-done.1
  100.8 1.3 collective-permute-start.2
  102.1 5.5 %collective-permute-start.3 = (bf16[64,1,256]{2,0,1:T(8,128)(2,1)S(1)}, bf16[64,1,256]{2,0,1:T(8,128)(2,1)S(1)}, u32[]{:S(2)}, u32[]{:S(2)}) collective-permute-start(bf16[64,1,256]{2,0,1:T(8,128)(2,1)S(1)} %get-tuple-element.483), channel_id=1, source_target_pairs={{0,1},{1,2},{2,3},{3,4},{4,5},{5,6},{6,7},{8,9},{9,10},{10,11},{11... | collective-permute-start | bytes 98312 | tf_op jit(solution)/shard_map/while/body/eval_jaxpr/ppermute | solution.py:19
  107.6 1.6 collective-permute-done.3
  109.3 0.6 fusion.555
  109.9 0.4 copy-done.2
  115.0 1.3 collective-permute-start.4
  116.3 3.7 %collective-permute-done.4 = bf16[64,4,256]{2,0,1:T(8,128)(2,1)S(1)} collective-permute-done((bf16[64,4,256]{2,0,1:T(8,128)(2,1)S(1)}, bf16[64,4,256]{2,0,1:T(8,128)(2,1)S(1)}, u32[]{:S(2)}, u32[]{:S(2)}) %collective-permute-start.4) | collective-permute-done | bytes 131104 | tf_op jit(solution)/shard_map/while/body/eval_jaxpr/ppermute | solution.py:30
  120.1 0.4 reduce_sum.19
  120.5 1.3 collective-permute-start
  121.8 5.4 %collective-permute-start.1 = (bf16[64,1,64]{0,2,1:T(8,128)(2,1)S(1)}, bf16[64,1,64]{0,2,1:T(8,128)(2,1)S(1)}, u32[]{:S(2)}, u32[]{:S(2)}) collective-permute-start(bf16[64,1,64]{0,2,1:T(8,128)(2,1)S(1)} %get-tuple-element.480), channel_id=1, source_target_pairs={{0,1},{1,2},{2,3},{3,4},{4,5},{5,6},{6,7},{8,9},{9,10},{10,11},{11... | collective-permute-start | bytes 24584 | tf_op jit(solution)/shard_map/while/body/eval_jaxpr/ppermute | solution.py:19
  127.3 1.4 collective-permute-done.1
  134.4 1.3 collective-permute-start.2
  135.7 5.5 %collective-permute-start.3 = (bf16[64,1,256]{2,0,1:T(8,128)(2,1)S(1)}, bf16[64,1,256]{2,0,1:T(8,128)(2,1)S(1)}, u32[]{:S(2)}, u32[]{:S(2)}) collective-permute-start(bf16[64,1,256]{2,0,1:T(8,128)(2,1)S(1)} %get-tuple-element.483), channel_id=1, source_target_pairs={{0,1},{1,2},{2,3},{3,4},{4,5},{5,6},{6,7},{8,9},{9,10},{10,11},{11... | collective-permute-start | bytes 98312 | tf_op jit(solution)/shard_map/while/body/eval_jaxpr/ppermute | solution.py:19
  141.2 1.6 collective-permute-done.3
  142.9 0.6 fusion.555
  143.5 0.4 copy-done.2
  148.6 1.3 collective-permute-start.4
  149.9 3.7 %collective-permute-done.4 = bf16[64,4,256]{2,0,1:T(8,128)(2,1)S(1)} collective-permute-done((bf16[64,4,256]{2,0,1:T(8,128)(2,1)S(1)}, bf16[64,4,256]{2,0,1:T(8,128)(2,1)S(1)}, u32[]{:S(2)}, u32[]{:S(2)}) %collective-permute-start.4) | collective-permute-done | bytes 131104 | tf_op jit(solution)/shard_map/while/body/eval_jaxpr/ppermute | solution.py:30
  153.7 0.2 slice_select_fusion.7
  158.8 0.2 fusion.176
  159.1 0.2 fusion.179
  160.0 0.2 fusion.181
  160.2 0.2 fusion.173
  160.5 0.2 fusion.174
  160.7 0.2 fusion.175
  165.5 1.0 copy.214
  166.8 0.9 pad_maximum_fusion.6
  167.7 0.8 copy.438
  168.5 84.0 %all-reduce.7.cloned.1.call-done = (bf16[27,64,64]{2,1,0:T(8,128)(2,1)}, bf16[27,64,64]{2,1,0:T(8,128)(2,1)}) async-done(((bf16[27,64,64]{2,1,0:T(8,128)(2,1)}, bf16[27,64,64]{2,1,0:T(8,128)(2,1)}), (bf16[27,64,64]{2,1,0:T(8,128)(2,1)}, bf16[27,64,64]{2,1,0:T(8,128)(2,1)})) %all-reduce.7.cloned.1.call-update) | async-done | bytes 442384 | tf_op jit(solution)/shard_map/psum | solution.py:194
  252.5 2.1 multiply_bitcast_fusion
  254.6 1.0 multiply_bitcast_fusion.1
  (381 shorter events, 52.3 us)
Async XLA Ops:
  7.2 151.7 %copy-start = (bf16[1,64,4,256]{3,2,1,0:T(4,128)(2,1)S(1)}, bf16[1,64,4,256]{3,2,1,0:T(4,128)(2,1)}, u32[]{:S(2)}) copy-start(bf16[1,64,4,256]{3,2,1,0:T(4,128)(2,1)} %param.14) | copy-start | bytes 393220
  7.2 0.9 copy-start.6
  7.2 10.6 %copy-start.4 = (bf16[1,64,4,256]{3,2,1,0:T(4,128)(2,1)S(1)}, bf16[1,64,4,256]{3,2,1,0:T(4,128)(2,1)}, u32[]{:S(2)}) copy-start(bf16[1,64,4,256]{3,2,1,0:T(4,128)(2,1)} %param.15) | copy-start | bytes 393220
  7.2 13.3 %copy-start.5 = (bf16[64,4,256]{2,1,0:T(4,128)(2,1)S(1)}, bf16[64,4,256]{2,1,0:T(4,128)(2,1)}, u32[]{:S(2)}) copy-start(bf16[64,4,256]{2,1,0:T(4,128)(2,1)} %param.11) | copy-start | bytes 393220
  7.2 15.8 %copy-start.1 = (bf16[1,27,64,64]{3,2,1,0:T(8,128)(2,1)S(1)}, bf16[1,27,64,64]{3,2,1,0:T(8,128)(2,1)}, u32[]{:S(2)}) copy-start(bf16[1,27,64,64]{3,2,1,0:T(8,128)(2,1)} %param.19) | copy-start | bytes 663556
  9.0 14.0 %all-to-all-start = ((bf16[128,16,1,8]{0,3,2,1:T(8,128)(2,1)}), bf16[128,16,1,8]{0,3,2,1:T(8,128)(2,1)S(1)}, u32[]{:S(2)}, u32[]{:S(2)}) async-start(bf16[128,16,1,8]{0,3,2,1:T(8,128)(2,1)} %maximum_bitcast_fusion.24), calls=%async_computation | async-start | bytes 65536 | tf_op jit(solution)/shard_map/all_to_all | solution.py:105
  16.2 236.3 %all-reduce.7.cloned.1.call-start = ((), (), s32[]{:S(2)}) async-start(), calls=%async_computation.1 | async-start | bytes 1769472 | tf_op jit(solution)/shard_map/psum | solution.py:194
  23.6 5.9 %collective-permute-start = (bf16[64,1,64]{0,2,1:T(8,128)(2,1)S(1)}, bf16[64,1,64]{0,2,1:T(8,128)(2,1)S(1)}, u32[]{:S(2)}, u32[]{:S(2)}) collective-permute-start(bf16[64,1,64]{0,2,1:T(8,128)(2,1)S(1)} %get-tuple-element.479), channel_id=1, source_target_pairs={{1,0},{2,1},{3,2},{4,3},{5,4},{6,5},{7,6},{9,8},{10,9},{11,10},{12... | collective-permute-start | bytes 24584 | tf_op jit(solution)/shard_map/while/body/eval_jaxpr/ppermute | solution.py:22
  24.9 6.0 %collective-permute-start.1 = (bf16[64,1,64]{0,2,1:T(8,128)(2,1)S(1)}, bf16[64,1,64]{0,2,1:T(8,128)(2,1)S(1)}, u32[]{:S(2)}, u32[]{:S(2)}) collective-permute-start(bf16[64,1,64]{0,2,1:T(8,128)(2,1)S(1)} %get-tuple-element.480), channel_id=1, source_target_pairs={{0,1},{1,2},{2,3},{3,4},{4,5},{5,6},{6,7},{8,9},{9,10},{10,11},{11... | collective-permute-start | bytes 24584 | tf_op jit(solution)/shard_map/while/body/eval_jaxpr/ppermute | solution.py:19
  36.6 6.2 %collective-permute-start.2 = (bf16[64,1,256]{2,0,1:T(8,128)(2,1)S(1)}, bf16[64,1,256]{2,0,1:T(8,128)(2,1)S(1)}, u32[]{:S(2)}, u32[]{:S(2)}) collective-permute-start(bf16[64,1,256]{2,0,1:T(8,128)(2,1)S(1)} %get-tuple-element.482), channel_id=1, source_target_pairs={{1,0},{2,1},{3,2},{4,3},{5,4},{6,5},{7,6},{9,8},{10,9},{11,10},{12... | collective-permute-start | bytes 98312 | tf_op jit(solution)/shard_map/while/body/eval_jaxpr/ppermute | solution.py:22
  37.9 6.4 %collective-permute-start.3 = (bf16[64,1,256]{2,0,1:T(8,128)(2,1)S(1)}, bf16[64,1,256]{2,0,1:T(8,128)(2,1)S(1)}, u32[]{:S(2)}, u32[]{:S(2)}) collective-permute-start(bf16[64,1,256]{2,0,1:T(8,128)(2,1)S(1)} %get-tuple-element.483), channel_id=1, source_target_pairs={{0,1},{1,2},{2,3},{3,4},{4,5},{5,6},{6,7},{8,9},{9,10},{10,11},{11... | collective-permute-start | bytes 98312 | tf_op jit(solution)/shard_map/while/body/eval_jaxpr/ppermute | solution.py:19
  44.5 1.0 copy-start.2
  50.2 3.2 %collective-permute-start.4 = (bf16[64,4,256]{2,0,1:T(8,128)(2,1)S(1)}, bf16[64,4,256]{2,0,1:T(8,128)(2,1)S(1)}, u32[]{:S(2)}, u32[]{:S(2)}) collective-permute-start(bf16[64,4,256]{2,0,1:T(8,128)(2,1)S(1)} %get-tuple-element.496), channel_id=1, source_target_pairs={{8,0},{16,8},{24,16},{9,1},{17,9},{25,17},{10,2},{18,10},{26,18},{... | collective-permute-start | bytes 393224 | tf_op jit(solution)/shard_map/while/body/eval_jaxpr/ppermute | solution.py:30
  54.0 6.8 %collective-permute-start = (bf16[64,1,64]{0,2,1:T(8,128)(2,1)S(1)}, bf16[64,1,64]{0,2,1:T(8,128)(2,1)S(1)}, u32[]{:S(2)}, u32[]{:S(2)}) collective-permute-start(bf16[64,1,64]{0,2,1:T(8,128)(2,1)S(1)} %get-tuple-element.479), channel_id=1, source_target_pairs={{1,0},{2,1},{3,2},{4,3},{5,4},{6,5},{7,6},{9,8},{10,9},{11,10},{12... | collective-permute-start | bytes 24584 | tf_op jit(solution)/shard_map/while/body/eval_jaxpr/ppermute | solution.py:22
  55.3 6.9 %collective-permute-start.1 = (bf16[64,1,64]{0,2,1:T(8,128)(2,1)S(1)}, bf16[64,1,64]{0,2,1:T(8,128)(2,1)S(1)}, u32[]{:S(2)}, u32[]{:S(2)}) collective-permute-start(bf16[64,1,64]{0,2,1:T(8,128)(2,1)S(1)} %get-tuple-element.480), channel_id=1, source_target_pairs={{0,1},{1,2},{2,3},{3,4},{4,5},{5,6},{6,7},{8,9},{9,10},{10,11},{11... | collective-permute-start | bytes 24584 | tf_op jit(solution)/shard_map/while/body/eval_jaxpr/ppermute | solution.py:19
  67.9 7.1 %collective-permute-start.2 = (bf16[64,1,256]{2,0,1:T(8,128)(2,1)S(1)}, bf16[64,1,256]{2,0,1:T(8,128)(2,1)S(1)}, u32[]{:S(2)}, u32[]{:S(2)}) collective-permute-start(bf16[64,1,256]{2,0,1:T(8,128)(2,1)S(1)} %get-tuple-element.482), channel_id=1, source_target_pairs={{1,0},{2,1},{3,2},{4,3},{5,4},{6,5},{7,6},{9,8},{10,9},{11,10},{12... | collective-permute-start | bytes 98312 | tf_op jit(solution)/shard_map/while/body/eval_jaxpr/ppermute | solution.py:22
  69.2 7.3 %collective-permute-start.3 = (bf16[64,1,256]{2,0,1:T(8,128)(2,1)S(1)}, bf16[64,1,256]{2,0,1:T(8,128)(2,1)S(1)}, u32[]{:S(2)}, u32[]{:S(2)}) collective-permute-start(bf16[64,1,256]{2,0,1:T(8,128)(2,1)S(1)} %get-tuple-element.483), channel_id=1, source_target_pairs={{0,1},{1,2},{2,3},{3,4},{4,5},{5,6},{6,7},{8,9},{9,10},{10,11},{11... | collective-permute-start | bytes 98312 | tf_op jit(solution)/shard_map/while/body/eval_jaxpr/ppermute | solution.py:19
  76.7 1.0 copy-start.2
  82.3 4.0 %collective-permute-start.4 = (bf16[64,4,256]{2,0,1:T(8,128)(2,1)S(1)}, bf16[64,4,256]{2,0,1:T(8,128)(2,1)S(1)}, u32[]{:S(2)}, u32[]{:S(2)}) collective-permute-start(bf16[64,4,256]{2,0,1:T(8,128)(2,1)S(1)} %get-tuple-element.496), channel_id=1, source_target_pairs={{8,0},{16,8},{24,16},{9,1},{17,9},{25,17},{10,2},{18,10},{26,18},{... | collective-permute-start | bytes 393224 | tf_op jit(solution)/shard_map/while/body/eval_jaxpr/ppermute | solution.py:30
  86.9 6.8 %collective-permute-start = (bf16[64,1,64]{0,2,1:T(8,128)(2,1)S(1)}, bf16[64,1,64]{0,2,1:T(8,128)(2,1)S(1)}, u32[]{:S(2)}, u32[]{:S(2)}) collective-permute-start(bf16[64,1,64]{0,2,1:T(8,128)(2,1)S(1)} %get-tuple-element.479), channel_id=1, source_target_pairs={{1,0},{2,1},{3,2},{4,3},{5,4},{6,5},{7,6},{9,8},{10,9},{11,10},{12... | collective-permute-start | bytes 24584 | tf_op jit(solution)/shard_map/while/body/eval_jaxpr/ppermute | solution.py:22
  88.2 6.9 %collective-permute-start.1 = (bf16[64,1,64]{0,2,1:T(8,128)(2,1)S(1)}, bf16[64,1,64]{0,2,1:T(8,128)(2,1)S(1)}, u32[]{:S(2)}, u32[]{:S(2)}) collective-permute-start(bf16[64,1,64]{0,2,1:T(8,128)(2,1)S(1)} %get-tuple-element.480), channel_id=1, source_target_pairs={{0,1},{1,2},{2,3},{3,4},{4,5},{5,6},{6,7},{8,9},{9,10},{10,11},{11... | collective-permute-start | bytes 24584 | tf_op jit(solution)/shard_map/while/body/eval_jaxpr/ppermute | solution.py:19
  100.8 6.8 %collective-permute-start.2 = (bf16[64,1,256]{2,0,1:T(8,128)(2,1)S(1)}, bf16[64,1,256]{2,0,1:T(8,128)(2,1)S(1)}, u32[]{:S(2)}, u32[]{:S(2)}) collective-permute-start(bf16[64,1,256]{2,0,1:T(8,128)(2,1)S(1)} %get-tuple-element.482), channel_id=1, source_target_pairs={{1,0},{2,1},{3,2},{4,3},{5,4},{6,5},{7,6},{9,8},{10,9},{11,10},{12... | collective-permute-start | bytes 98312 | tf_op jit(solution)/shard_map/while/body/eval_jaxpr/ppermute | solution.py:22
  102.1 7.0 %collective-permute-start.3 = (bf16[64,1,256]{2,0,1:T(8,128)(2,1)S(1)}, bf16[64,1,256]{2,0,1:T(8,128)(2,1)S(1)}, u32[]{:S(2)}, u32[]{:S(2)}) collective-permute-start(bf16[64,1,256]{2,0,1:T(8,128)(2,1)S(1)} %get-tuple-element.483), channel_id=1, source_target_pairs={{0,1},{1,2},{2,3},{3,4},{4,5},{5,6},{6,7},{8,9},{9,10},{10,11},{11... | collective-permute-start | bytes 98312 | tf_op jit(solution)/shard_map/while/body/eval_jaxpr/ppermute | solution.py:19
  109.3 1.0 copy-start.2
  115.0 5.0 %collective-permute-start.4 = (bf16[64,4,256]{2,0,1:T(8,128)(2,1)S(1)}, bf16[64,4,256]{2,0,1:T(8,128)(2,1)S(1)}, u32[]{:S(2)}, u32[]{:S(2)}) collective-permute-start(bf16[64,4,256]{2,0,1:T(8,128)(2,1)S(1)} %get-tuple-element.496), channel_id=1, source_target_pairs={{8,0},{16,8},{24,16},{9,1},{17,9},{25,17},{10,2},{18,10},{26,18},{... | collective-permute-start | bytes 393224 | tf_op jit(solution)/shard_map/while/body/eval_jaxpr/ppermute | solution.py:30
  120.5 6.8 %collective-permute-start = (bf16[64,1,64]{0,2,1:T(8,128)(2,1)S(1)}, bf16[64,1,64]{0,2,1:T(8,128)(2,1)S(1)}, u32[]{:S(2)}, u32[]{:S(2)}) collective-permute-start(bf16[64,1,64]{0,2,1:T(8,128)(2,1)S(1)} %get-tuple-element.479), channel_id=1, source_target_pairs={{1,0},{2,1},{3,2},{4,3},{5,4},{6,5},{7,6},{9,8},{10,9},{11,10},{12... | collective-permute-start | bytes 24584 | tf_op jit(solution)/shard_map/while/body/eval_jaxpr/ppermute | solution.py:22
  121.8 6.9 %collective-permute-start.1 = (bf16[64,1,64]{0,2,1:T(8,128)(2,1)S(1)}, bf16[64,1,64]{0,2,1:T(8,128)(2,1)S(1)}, u32[]{:S(2)}, u32[]{:S(2)}) collective-permute-start(bf16[64,1,64]{0,2,1:T(8,128)(2,1)S(1)} %get-tuple-element.480), channel_id=1, source_target_pairs={{0,1},{1,2},{2,3},{3,4},{4,5},{5,6},{6,7},{8,9},{9,10},{10,11},{11... | collective-permute-start | bytes 24584 | tf_op jit(solution)/shard_map/while/body/eval_jaxpr/ppermute | solution.py:19
  134.4 6.8 %collective-permute-start.2 = (bf16[64,1,256]{2,0,1:T(8,128)(2,1)S(1)}, bf16[64,1,256]{2,0,1:T(8,128)(2,1)S(1)}, u32[]{:S(2)}, u32[]{:S(2)}) collective-permute-start(bf16[64,1,256]{2,0,1:T(8,128)(2,1)S(1)} %get-tuple-element.482), channel_id=1, source_target_pairs={{1,0},{2,1},{3,2},{4,3},{5,4},{6,5},{7,6},{9,8},{10,9},{11,10},{12... | collective-permute-start | bytes 98312 | tf_op jit(solution)/shard_map/while/body/eval_jaxpr/ppermute | solution.py:22
  135.7 7.0 %collective-permute-start.3 = (bf16[64,1,256]{2,0,1:T(8,128)(2,1)S(1)}, bf16[64,1,256]{2,0,1:T(8,128)(2,1)S(1)}, u32[]{:S(2)}, u32[]{:S(2)}) collective-permute-start(bf16[64,1,256]{2,0,1:T(8,128)(2,1)S(1)} %get-tuple-element.483), channel_id=1, source_target_pairs={{0,1},{1,2},{2,3},{3,4},{4,5},{5,6},{6,7},{8,9},{9,10},{10,11},{11... | collective-permute-start | bytes 98312 | tf_op jit(solution)/shard_map/while/body/eval_jaxpr/ppermute | solution.py:19
  142.9 1.0 copy-start.2
  148.6 5.0 %collective-permute-start.4 = (bf16[64,4,256]{2,0,1:T(8,128)(2,1)S(1)}, bf16[64,4,256]{2,0,1:T(8,128)(2,1)S(1)}, u32[]{:S(2)}, u32[]{:S(2)}) collective-permute-start(bf16[64,4,256]{2,0,1:T(8,128)(2,1)S(1)} %get-tuple-element.496), channel_id=1, source_target_pairs={{8,0},{16,8},{24,16},{9,1},{17,9},{25,17},{10,2},{18,10},{26,18},{... | collective-permute-start | bytes 393224 | tf_op jit(solution)/shard_map/while/body/eval_jaxpr/ppermute | solution.py:30
  252.5 2.1 copy-start.3
Sparse Core Ops, SparseCore 0:
  167.8 84.6 all-reduce.6
where the time goes:
time: 263 us; the launch traced here: 262 us
  waiting for transfers between devices  110 us (42%)
  starting transfers between devices  65.2 us (25%)
  matrix products  49.5 us (19%)
  between operations  14.6 us (6%)
  other arithmetic  13.4 us (5%)
  local copies, waits for them, and re-layouts  7.91 us (3%)
    psum x1, waiting for transfers between devices, on_device(): lax.psum(fine_local.astype(jnp.bfloat16), 'vol').astype(jnp.float32)  84 us
    ppermute x8, starting transfers between devices, padded_2(): lax.ppermute(lax.slice_in_dim(block, block.shape[dim] - width, None, axis...  42.3 us
    dot_general x216, matrix products, back_sum(): jnp.einsum('io,orp->irp', kernel[tap_key], pieces[tap_key], preferred_ele...  38.6 us
    ppermute x4, waiting for transfers between devices, from_behind(): return lax.ppermute(array, axis, pairs)  12 us
    ppermute x8, waiting for transfers between devices, padded_2(): lax.ppermute(lax.slice_in_dim(block, block.shape[dim] - width, None, axis...  11.6 us
    dot_general x54, matrix products, filter_grid(): jnp.einsum('irp,orp->io', saved_local, pieces[outer_tap, middle_tap, inne...  10.9 us
    ppermute x8, starting transfers between devices, padded_2(): lax.ppermute(lax.slice_in_dim(block, 0, width, axis=dim), axis, backward)  10.3 us
    all_to_all x1, starting transfers between devices, to_depth(): lax.all_to_all(shortened(shaped), 'vol', split_axis=1, concat_axis=2, til...  7.28 us
  transfers between devices with their start and end apart: 22, of which 14 were waited for; matrix products, arithmetic and copies ran while one was open for 2% of the time, Pallas kernels for 0%

commit v1 on v0

--- a/solution.py
+++ b/solution.py
@@ -191,7 +191,7 @@
     fine_local = filter_grid(tap_pieces(finished[2], XL), saved_input)
     coarse_local = filter_grid(tap_pieces(finished[3], half_cols), coarse_saved)
     fine_total, coarse_total = (
-        lax.psum(fine_local.astype(jnp.bfloat16), "vol").astype(jnp.float32),
+        jnp.sum(lax.all_gather(fine_local.astype(jnp.bfloat16), "vol"), axis=0).astype(jnp.float32),
         lax.psum(coarse_local.astype(jnp.bfloat16), "vol").astype(jnp.float32),
     )
     fine_cells = depth_len * vol_count * plane_len

time: 263 us -> 357 us (1.36); the launches traced: 262 us -> 353 us
  waiting for transfers between devices: 110 us -> 167 us
  matrix products: 49.5 us -> 78.2 us
  other arithmetic: 13.4 us -> 17 us
    all_gather x0 -> x1, waiting for transfers between devices: none -> 64.5 us  [on_device(): lax.all_gather(fine_local.astype(jnp.bfloat16), 'vol')]
    dot_general x216, matrix products: 38.6 us -> 67.4 us  [back_sum(): jnp.einsum('io,orp->irp', kernel[tap_key], pieces[tap_key], preferred_ele...]
    psum x1, waiting for transfers between devices: 84 us -> 78.5 us  [on_device(): lax.psum(coarse_local.astype(jnp.bfloat16), 'vol').astype(jnp.float32)]
  transfers between devices with their start and end apart: 22 -> 23, of which waited for: 14 -> 15; matrix products, arithmetic and copies ran while one was open for 2% -> 3% of each run, Pallas kernels for 0% -> 0%
where the time goes in v1:
time: 357 us; the launch traced here: 353 us
  waiting for transfers between devices  167 us (47%)
  matrix products  78.2 us (22%)
  starting transfers between devices  65.4 us (18%)
  other arithmetic  17 us (5%)
  between operations  14.5 us (4%)
  local copies, waits for them, and re-layouts  8.43 us (2%)
    psum x1, waiting for transfers between devices, on_device(): lax.psum(coarse_local.astype(jnp.bfloat16), 'vol').astype(jnp.float32)  78.5 us
    dot_general x216, matrix products, back_sum(): jnp.einsum('io,orp->irp', kernel[tap_key], pieces[tap_key], preferred_ele...  67.4 us
    all_gather x1, waiting for transfers between devices, on_device(): lax.all_gather(fine_local.astype(jnp.bfloat16), 'vol')  64.5 us
    ppermute x8, starting transfers between devices, padded_2(): lax.ppermute(lax.slice_in_dim(block, block.shape[dim] - width, None, axis...  42.6 us
    ppermute x4, waiting for transfers between devices, from_behind(): return lax.ppermute(array, axis, pairs)  12 us
    ppermute x8, waiting for transfers between devices, padded_2(): lax.ppermute(lax.slice_in_dim(block, block.shape[dim] - width, None, axis...  11.6 us
    dot_general x54, matrix products, filter_grid(): jnp.einsum('irp,orp->io', saved_local, pieces[outer_tap, middle_tap, inne...  10.9 us
    ppermute x8, starting transfers between devices, padded_2(): lax.ppermute(lax.slice_in_dim(block, 0, width, axis=dim), axis, backward)  10.3 us
  transfers between devices with their start and end apart: 23, of which 15 were waited for; matrix products, arithmetic and copies ran while one was open for 3% of the time, Pallas kernels for 0%

profile of v1, /device:TPU:0, one launch (start us, length us, event | category | flops | bytes accessed | tf_op | source)
XLA Modules:
  0.0 352.8 jit_solution(8518883094440890618)
XLA Ops:
  9.6 7.3 %all-to-all-start = ((bf16[128,16,1,8]{0,3,2,1:T(8,128)(2,1)}), bf16[128,16,1,8]{0,3,2,1:T(8,128)(2,1)S(1)}, u32[]{:S(2)}, u32[]{:S(2)}) async-start(bf16[128,16,1,8]{0,3,2,1:T(8,128)(2,1)} %maximum_bitcast_fusion.24), calls=%async_computation | async-start | bytes 65536 | tf_op jit(solution)/shard_map/all_to_all | solution.py:105
  17.0 1.4 fusion.382
  18.4 1.0 compare_bitcast_fusion
  19.4 2.6 select_add_fusion
  22.0 0.9 fusion.217
  23.6 158.0 %while.23 = (s32[]{:T(128)}, bf16[64,4,256]{2,0,1:T(8,128)(2,1)S(1)}, bf16[64,4,256]{2,0,1:T(8,128)(2,1)S(1)}, bf16[64,6,256]{2,0,1:T(8,128)(2,1)S(1)}, bf16[64,...) while((s32[]{:T(128)}, ...), condition=%wide.region_2.3_spmd.clone, body=%wide.region_0.2_spmd.clone.sunk | while | flops 259488704 | bytes 30150104 | solution.py:189
  24.2 1.3 collective-permute-start
  25.5 4.5 %collective-permute-start.1 = (bf16[64,1,64]{0,2,1:T(8,128)(2,1)S(1)}, bf16[64,1,64]{0,2,1:T(8,128)(2,1)S(1)}, u32[]{:S(2)}, u32[]{:S(2)}) collective-permute-start(bf16[64,1,64]{0,2,1:T(8,128)(2,1)S(1)} %get-tuple-element.481), channel_id=1, source_target_pairs={{0,1},{1,2},{2,3},{3,4},{4,5},{5,6},{6,7},{8,9},{9,10},{10,11},{11... | collective-permute-start | bytes 24584 | tf_op jit(solution)/shard_map/while/body/eval_jaxpr/ppermute | solution.py:19
  30.2 1.4 collective-permute-done.1
  34.3 0.9 convolution_add_fusion.56
  35.2 0.9 convolution_add_fusion.57
  36.1 0.9 convolution_add_fusion.58
  37.0 0.9 fusion.541
  37.9 0.9 convolution_add_fusion.59
  44.5 1.3 collective-permute-start.2
  45.8 4.8 %collective-permute-start.3 = (bf16[64,1,256]{2,0,1:T(8,128)(2,1)S(1)}, bf16[64,1,256]{2,0,1:T(8,128)(2,1)S(1)}, u32[]{:S(2)}, u32[]{:S(2)}) collective-permute-start(bf16[64,1,256]{2,0,1:T(8,128)(2,1)S(1)} %get-tuple-element.484), channel_id=1, source_target_pairs={{0,1},{1,2},{2,3},{3,4},{4,5},{5,6},{6,7},{8,9},{9,10},{10,11},{11... | collective-permute-start | bytes 98312 | tf_op jit(solution)/shard_map/while/body/eval_jaxpr/ppermute | solution.py:19
  50.6 1.6 collective-permute-done.3
  57.6 1.3 collective-permute-start.4
  58.9 1.9 collective-permute-done.4
  61.4 1.3 collective-permute-start
  62.7 5.7 %collective-permute-start.1 = (bf16[64,1,64]{0,2,1:T(8,128)(2,1)S(1)}, bf16[64,1,64]{0,2,1:T(8,128)(2,1)S(1)}, u32[]{:S(2)}, u32[]{:S(2)}) collective-permute-start(bf16[64,1,64]{0,2,1:T(8,128)(2,1)S(1)} %get-tuple-element.481), channel_id=1, source_target_pairs={{0,1},{1,2},{2,3},{3,4},{4,5},{5,6},{6,7},{8,9},{9,10},{10,11},{11... | collective-permute-start | bytes 24584 | tf_op jit(solution)/shard_map/while/body/eval_jaxpr/ppermute | solution.py:19
  68.4 1.4 collective-permute-done.1
  72.6 0.9 convolution_add_fusion.56
  73.5 0.9 convolution_add_fusion.57
  74.4 0.9 convolution_add_fusion.58
  75.3 0.9 fusion.541
  76.2 0.9 convolution_add_fusion.59
  82.7 1.3 collective-permute-start.2
  84.0 5.7 %collective-permute-start.3 = (bf16[64,1,256]{2,0,1:T(8,128)(2,1)S(1)}, bf16[64,1,256]{2,0,1:T(8,128)(2,1)S(1)}, u32[]{:S(2)}, u32[]{:S(2)}) collective-permute-start(bf16[64,1,256]{2,0,1:T(8,128)(2,1)S(1)} %get-tuple-element.484), channel_id=1, source_target_pairs={{0,1},{1,2},{2,3},{3,4},{4,5},{5,6},{6,7},{8,9},{9,10},{10,11},{11... | collective-permute-start | bytes 98312 | tf_op jit(solution)/shard_map/while/body/eval_jaxpr/ppermute | solution.py:19
  89.8 1.6 collective-permute-done.3
  96.8 1.3 collective-permute-start.4
  98.1 2.7 collective-permute-done.4
  101.3 1.3 collective-permute-start
  102.6 5.4 %collective-permute-start.1 = (bf16[64,1,64]{0,2,1:T(8,128)(2,1)S(1)}, bf16[64,1,64]{0,2,1:T(8,128)(2,1)S(1)}, u32[]{:S(2)}, u32[]{:S(2)}) collective-permute-start(bf16[64,1,64]{0,2,1:T(8,128)(2,1)S(1)} %get-tuple-element.481), channel_id=1, source_target_pairs={{0,1},{1,2},{2,3},{3,4},{4,5},{5,6},{6,7},{8,9},{9,10},{10,11},{11... | collective-permute-start | bytes 24584 | tf_op jit(solution)/shard_map/while/body/eval_jaxpr/ppermute | solution.py:19
  108.2 1.4 collective-permute-done.1
  112.3 0.9 convolution_add_fusion.56
  113.2 0.9 convolution_add_fusion.57
  114.1 0.9 convolution_add_fusion.58
  115.0 0.9 fusion.541
  115.9 0.9 convolution_add_fusion.59
  122.5 1.3 collective-permute-start.2
  123.8 5.5 %collective-permute-start.3 = (bf16[64,1,256]{2,0,1:T(8,128)(2,1)S(1)}, bf16[64,1,256]{2,0,1:T(8,128)(2,1)S(1)}, u32[]{:S(2)}, u32[]{:S(2)}) collective-permute-start(bf16[64,1,256]{2,0,1:T(8,128)(2,1)S(1)} %get-tuple-element.484), channel_id=1, source_target_pairs={{0,1},{1,2},{2,3},{3,4},{4,5},{5,6},{6,7},{8,9},{9,10},{10,11},{11... | collective-permute-start | bytes 98312 | tf_op jit(solution)/shard_map/while/body/eval_jaxpr/ppermute | solution.py:19
  129.2 1.6 collective-permute-done.3
  136.2 1.3 collective-permute-start.4
  137.5 3.7 %collective-permute-done.4 = bf16[64,4,256]{2,0,1:T(8,128)(2,1)S(1)} collective-permute-done((bf16[64,4,256]{2,0,1:T(8,128)(2,1)S(1)}, bf16[64,4,256]{2,0,1:T(8,128)(2,1)S(1)}, u32[]{:S(2)}, u32[]{:S(2)}) %collective-permute-start.4) | collective-permute-done | bytes 131104 | tf_op jit(solution)/shard_map/while/body/eval_jaxpr/ppermute | solution.py:30
  141.8 1.3 collective-permute-start
  143.1 5.4 %collective-permute-start.1 = (bf16[64,1,64]{0,2,1:T(8,128)(2,1)S(1)}, bf16[64,1,64]{0,2,1:T(8,128)(2,1)S(1)}, u32[]{:S(2)}, u32[]{:S(2)}) collective-permute-start(bf16[64,1,64]{0,2,1:T(8,128)(2,1)S(1)} %get-tuple-element.481), channel_id=1, source_target_pairs={{0,1},{1,2},{2,3},{3,4},{4,5},{5,6},{6,7},{8,9},{9,10},{10,11},{11... | collective-permute-start | bytes 24584 | tf_op jit(solution)/shard_map/while/body/eval_jaxpr/ppermute | solution.py:19
  148.6 1.4 collective-permute-done.1
  152.7 0.9 convolution_add_fusion.56
  153.6 0.9 convolution_add_fusion.57
  154.5 0.9 convolution_add_fusion.58
  155.5 0.9 fusion.541
  156.4 0.9 convolution_add_fusion.59
  162.9 1.3 collective-permute-start.2
  164.2 5.5 %collective-permute-start.3 = (bf16[64,1,256]{2,0,1:T(8,128)(2,1)S(1)}, bf16[64,1,256]{2,0,1:T(8,128)(2,1)S(1)}, u32[]{:S(2)}, u32[]{:S(2)}) collective-permute-start(bf16[64,1,256]{2,0,1:T(8,128)(2,1)S(1)} %get-tuple-element.484), channel_id=1, source_target_pairs={{0,1},{1,2},{2,3},{3,4},{4,5},{5,6},{6,7},{8,9},{9,10},{10,11},{11... | collective-permute-start | bytes 98312 | tf_op jit(solution)/shard_map/while/body/eval_jaxpr/ppermute | solution.py:19
  169.7 1.6 collective-permute-done.3
  176.6 1.3 collective-permute-start.4
  178.0 3.7 %collective-permute-done.4 = bf16[64,4,256]{2,0,1:T(8,128)(2,1)S(1)} collective-permute-done((bf16[64,4,256]{2,0,1:T(8,128)(2,1)S(1)}, bf16[64,4,256]{2,0,1:T(8,128)(2,1)S(1)}, u32[]{:S(2)}, u32[]{:S(2)}) %collective-permute-start.4) | collective-permute-done | bytes 131104 | tf_op jit(solution)/shard_map/while/body/eval_jaxpr/ppermute | solution.py:30
  194.8 1.0 copy.211
  196.6 78.5 %all-reduce.6.cloned.1.call-done = bf16[27,64,64]{2,1,0:T(8,128)(2,1)} async-done(((bf16[27,64,64]{2,1,0:T(8,128)(2,1)}), bf16[27,64,64]{2,1,0:T(8,128)(2,1)}) %all-reduce.6.cloned.1.call-update) | async-done | bytes 221200 | tf_op jit(solution)/shard_map/psum | solution.py:195
  275.1 2.0 multiply_bitcast_fusion
  277.1 64.5 %all-gather.2.cloned.1.call-done = bf16[8,27,64,64]{3,2,1,0:T(8,128)(2,1)} async-done(((bf16[1,27,64,64]{3,2,1,0:T(8,128)(2,1)}), bf16[8,27,64,64]{3,2,1,0:T(8,128)(2,1)}) %all-gather.2.cloned.1.call-update) | async-done | bytes 1769488 | tf_op jit(solution)/shard_map/all_gather | solution.py:194
  341.6 2.8 reduce_sum.29
  344.7 1.2 copy.243
  (385 shorter events, 73.2 us)
Async XLA Ops:
  7.2 174.5 %copy-start = (bf16[1,64,4,256]{3,2,1,0:T(4,128)(2,1)S(1)}, bf16[1,64,4,256]{3,2,1,0:T(4,128)(2,1)}, u32[]{:S(2)}) copy-start(bf16[1,64,4,256]{3,2,1,0:T(4,128)(2,1)} %param.14) | copy-start | bytes 393220
  9.6 14.0 %all-to-all-start = ((bf16[128,16,1,8]{0,3,2,1:T(8,128)(2,1)}), bf16[128,16,1,8]{0,3,2,1:T(8,128)(2,1)S(1)}, u32[]{:S(2)}, u32[]{:S(2)}) async-start(bf16[128,16,1,8]{0,3,2,1:T(8,128)(2,1)} %maximum_bitcast_fusion.24), calls=%async_computation | async-start | bytes 65536 | tf_op jit(solution)/shard_map/all_to_all | solution.py:105
  16.9 258.2 %all-reduce.6.cloned.1.call-start = ((), (), s32[]{:S(2)}) async-start(), calls=%async_computation.2 | async-start | bytes 884736 | tf_op jit(solution)/shard_map/psum | solution.py:195
  23.7 17.0 %copy-start.1 = (bf16[1,27,64,64]{3,2,1,0:T(8,128)(2,1)S(1)}, bf16[1,27,64,64]{3,2,1,0:T(8,128)(2,1)}, u32[]{:S(2)}) copy-start(bf16[1,27,64,64]{3,2,1,0:T(8,128)(2,1)} %get-tuple-element.533) | copy-start | bytes 663556 | tf_op jit(solution)/shard_map/while
  24.2 5.9 %collective-permute-start = (bf16[64,1,64]{0,2,1:T(8,128)(2,1)S(1)}, bf16[64,1,64]{0,2,1:T(8,128)(2,1)S(1)}, u32[]{:S(2)}, u32[]{:S(2)}) collective-permute-start(bf16[64,1,64]{0,2,1:T(8,128)(2,1)S(1)} %get-tuple-element.480), channel_id=1, source_target_pairs={{1,0},{2,1},{3,2},{4,3},{5,4},{6,5},{7,6},{9,8},{10,9},{11,10},{12... | collective-permute-start | bytes 24584 | tf_op jit(solution)/shard_map/while/body/eval_jaxpr/ppermute | solution.py:22
  25.5 6.0 %collective-permute-start.1 = (bf16[64,1,64]{0,2,1:T(8,128)(2,1)S(1)}, bf16[64,1,64]{0,2,1:T(8,128)(2,1)S(1)}, u32[]{:S(2)}, u32[]{:S(2)}) collective-permute-start(bf16[64,1,64]{0,2,1:T(8,128)(2,1)S(1)} %get-tuple-element.481), channel_id=1, source_target_pairs={{0,1},{1,2},{2,3},{3,4},{4,5},{5,6},{6,7},{8,9},{9,10},{10,11},{11... | collective-permute-start | bytes 24584 | tf_op jit(solution)/shard_map/while/body/eval_jaxpr/ppermute | solution.py:19
  42.1 10.8 %copy-start.2 = (bf16[1,27,64,64]{3,2,1,0:T(8,128)(2,1)S(1)}, bf16[1,27,64,64]{3,2,1,0:T(8,128)(2,1)}, u32[]{:S(2)}) copy-start(bf16[1,27,64,64]{3,2,1,0:T(8,128)(2,1)} %get-tuple-element.535) | copy-start | bytes 663556 | tf_op jit(solution)/shard_map/while
  44.5 6.2 %collective-permute-start.2 = (bf16[64,1,256]{2,0,1:T(8,128)(2,1)S(1)}, bf16[64,1,256]{2,0,1:T(8,128)(2,1)S(1)}, u32[]{:S(2)}, u32[]{:S(2)}) collective-permute-start(bf16[64,1,256]{2,0,1:T(8,128)(2,1)S(1)} %get-tuple-element.483), channel_id=1, source_target_pairs={{1,0},{2,1},{3,2},{4,3},{5,4},{6,5},{7,6},{9,8},{10,9},{11,10},{12... | collective-permute-start | bytes 98312 | tf_op jit(solution)/shard_map/while/body/eval_jaxpr/ppermute | solution.py:22
  45.8 6.4 %collective-permute-start.3 = (bf16[64,1,256]{2,0,1:T(8,128)(2,1)S(1)}, bf16[64,1,256]{2,0,1:T(8,128)(2,1)S(1)}, u32[]{:S(2)}, u32[]{:S(2)}) collective-permute-start(bf16[64,1,256]{2,0,1:T(8,128)(2,1)S(1)} %get-tuple-element.484), channel_id=1, source_target_pairs={{0,1},{1,2},{2,3},{3,4},{4,5},{5,6},{6,7},{8,9},{9,10},{10,11},{11... | collective-permute-start | bytes 98312 | tf_op jit(solution)/shard_map/while/body/eval_jaxpr/ppermute | solution.py:19
  57.6 3.2 collective-permute-start.4
  60.8 18.1 %copy-start.1 = (bf16[1,27,64,64]{3,2,1,0:T(8,128)(2,1)S(1)}, bf16[1,27,64,64]{3,2,1,0:T(8,128)(2,1)}, u32[]{:S(2)}) copy-start(bf16[1,27,64,64]{3,2,1,0:T(8,128)(2,1)} %get-tuple-element.533) | copy-start | bytes 663556 | tf_op jit(solution)/shard_map/while
  61.4 7.0 %collective-permute-start = (bf16[64,1,64]{0,2,1:T(8,128)(2,1)S(1)}, bf16[64,1,64]{0,2,1:T(8,128)(2,1)S(1)}, u32[]{:S(2)}, u32[]{:S(2)}) collective-permute-start(bf16[64,1,64]{0,2,1:T(8,128)(2,1)S(1)} %get-tuple-element.480), channel_id=1, source_target_pairs={{1,0},{2,1},{3,2},{4,3},{5,4},{6,5},{7,6},{9,8},{10,9},{11,10},{12... | collective-permute-start | bytes 24584 | tf_op jit(solution)/shard_map/while/body/eval_jaxpr/ppermute | solution.py:22
  62.7 7.1 %collective-permute-start.1 = (bf16[64,1,64]{0,2,1:T(8,128)(2,1)S(1)}, bf16[64,1,64]{0,2,1:T(8,128)(2,1)S(1)}, u32[]{:S(2)}, u32[]{:S(2)}) collective-permute-start(bf16[64,1,64]{0,2,1:T(8,128)(2,1)S(1)} %get-tuple-element.481), channel_id=1, source_target_pairs={{0,1},{1,2},{2,3},{3,4},{4,5},{5,6},{6,7},{8,9},{9,10},{10,11},{11... | collective-permute-start | bytes 24584 | tf_op jit(solution)/shard_map/while/body/eval_jaxpr/ppermute | solution.py:19
  80.3 11.8 %copy-start.2 = (bf16[1,27,64,64]{3,2,1,0:T(8,128)(2,1)S(1)}, bf16[1,27,64,64]{3,2,1,0:T(8,128)(2,1)}, u32[]{:S(2)}) copy-start(bf16[1,27,64,64]{3,2,1,0:T(8,128)(2,1)} %get-tuple-element.535) | copy-start | bytes 663556 | tf_op jit(solution)/shard_map/while
  82.7 7.1 %collective-permute-start.2 = (bf16[64,1,256]{2,0,1:T(8,128)(2,1)S(1)}, bf16[64,1,256]{2,0,1:T(8,128)(2,1)S(1)}, u32[]{:S(2)}, u32[]{:S(2)}) collective-permute-start(bf16[64,1,256]{2,0,1:T(8,128)(2,1)S(1)} %get-tuple-element.483), channel_id=1, source_target_pairs={{1,0},{2,1},{3,2},{4,3},{5,4},{6,5},{7,6},{9,8},{10,9},{11,10},{12... | collective-permute-start | bytes 98312 | tf_op jit(solution)/shard_map/while/body/eval_jaxpr/ppermute | solution.py:22
  84.0 7.3 %collective-permute-start.3 = (bf16[64,1,256]{2,0,1:T(8,128)(2,1)S(1)}, bf16[64,1,256]{2,0,1:T(8,128)(2,1)S(1)}, u32[]{:S(2)}, u32[]{:S(2)}) collective-permute-start(bf16[64,1,256]{2,0,1:T(8,128)(2,1)S(1)} %get-tuple-element.484), channel_id=1, source_target_pairs={{0,1},{1,2},{2,3},{3,4},{4,5},{5,6},{6,7},{8,9},{9,10},{10,11},{11... | collective-permute-start | bytes 98312 | tf_op jit(solution)/shard_map/while/body/eval_jaxpr/ppermute | solution.py:19
  96.8 4.0 %collective-permute-start.4 = (bf16[64,4,256]{2,0,1:T(8,128)(2,1)S(1)}, bf16[64,4,256]{2,0,1:T(8,128)(2,1)S(1)}, u32[]{:S(2)}, u32[]{:S(2)}) collective-permute-start(bf16[64,4,256]{2,0,1:T(8,128)(2,1)S(1)} %get-tuple-element.497), channel_id=1, source_target_pairs={{8,0},{16,8},{24,16},{9,1},{17,9},{25,17},{10,2},{18,10},{26,18},{... | collective-permute-start | bytes 393224 | tf_op jit(solution)/shard_map/while/body/eval_jaxpr/ppermute | solution.py:30
  100.8 17.9 %copy-start.1 = (bf16[1,27,64,64]{3,2,1,0:T(8,128)(2,1)S(1)}, bf16[1,27,64,64]{3,2,1,0:T(8,128)(2,1)}, u32[]{:S(2)}) copy-start(bf16[1,27,64,64]{3,2,1,0:T(8,128)(2,1)} %get-tuple-element.533) | copy-start | bytes 663556 | tf_op jit(solution)/shard_map/while
  101.3 6.8 %collective-permute-start = (bf16[64,1,64]{0,2,1:T(8,128)(2,1)S(1)}, bf16[64,1,64]{0,2,1:T(8,128)(2,1)S(1)}, u32[]{:S(2)}, u32[]{:S(2)}) collective-permute-start(bf16[64,1,64]{0,2,1:T(8,128)(2,1)S(1)} %get-tuple-element.480), channel_id=1, source_target_pairs={{1,0},{2,1},{3,2},{4,3},{5,4},{6,5},{7,6},{9,8},{10,9},{11,10},{12... | collective-permute-start | bytes 24584 | tf_op jit(solution)/shard_map/while/body/eval_jaxpr/ppermute | solution.py:22
  102.6 6.9 %collective-permute-start.1 = (bf16[64,1,64]{0,2,1:T(8,128)(2,1)S(1)}, bf16[64,1,64]{0,2,1:T(8,128)(2,1)S(1)}, u32[]{:S(2)}, u32[]{:S(2)}) collective-permute-start(bf16[64,1,64]{0,2,1:T(8,128)(2,1)S(1)} %get-tuple-element.481), channel_id=1, source_target_pairs={{0,1},{1,2},{2,3},{3,4},{4,5},{5,6},{6,7},{8,9},{9,10},{10,11},{11... | collective-permute-start | bytes 24584 | tf_op jit(solution)/shard_map/while/body/eval_jaxpr/ppermute | solution.py:19
  120.0 11.5 %copy-start.2 = (bf16[1,27,64,64]{3,2,1,0:T(8,128)(2,1)S(1)}, bf16[1,27,64,64]{3,2,1,0:T(8,128)(2,1)}, u32[]{:S(2)}) copy-start(bf16[1,27,64,64]{3,2,1,0:T(8,128)(2,1)} %get-tuple-element.535) | copy-start | bytes 663556 | tf_op jit(solution)/shard_map/while
  122.5 6.8 %collective-permute-start.2 = (bf16[64,1,256]{2,0,1:T(8,128)(2,1)S(1)}, bf16[64,1,256]{2,0,1:T(8,128)(2,1)S(1)}, u32[]{:S(2)}, u32[]{:S(2)}) collective-permute-start(bf16[64,1,256]{2,0,1:T(8,128)(2,1)S(1)} %get-tuple-element.483), channel_id=1, source_target_pairs={{1,0},{2,1},{3,2},{4,3},{5,4},{6,5},{7,6},{9,8},{10,9},{11,10},{12... | collective-permute-start | bytes 98312 | tf_op jit(solution)/shard_map/while/body/eval_jaxpr/ppermute | solution.py:22
  123.8 7.0 %collective-permute-start.3 = (bf16[64,1,256]{2,0,1:T(8,128)(2,1)S(1)}, bf16[64,1,256]{2,0,1:T(8,128)(2,1)S(1)}, u32[]{:S(2)}, u32[]{:S(2)}) collective-permute-start(bf16[64,1,256]{2,0,1:T(8,128)(2,1)S(1)} %get-tuple-element.484), channel_id=1, source_target_pairs={{0,1},{1,2},{2,3},{3,4},{4,5},{5,6},{6,7},{8,9},{9,10},{10,11},{11... | collective-permute-start | bytes 98312 | tf_op jit(solution)/shard_map/while/body/eval_jaxpr/ppermute | solution.py:19
  136.2 5.0 %collective-permute-start.4 = (bf16[64,4,256]{2,0,1:T(8,128)(2,1)S(1)}, bf16[64,4,256]{2,0,1:T(8,128)(2,1)S(1)}, u32[]{:S(2)}, u32[]{:S(2)}) collective-permute-start(bf16[64,4,256]{2,0,1:T(8,128)(2,1)S(1)} %get-tuple-element.497), channel_id=1, source_target_pairs={{8,0},{16,8},{24,16},{9,1},{17,9},{25,17},{10,2},{18,10},{26,18},{... | collective-permute-start | bytes 393224 | tf_op jit(solution)/shard_map/while/body/eval_jaxpr/ppermute | solution.py:30
  141.2 17.9 %copy-start.1 = (bf16[1,27,64,64]{3,2,1,0:T(8,128)(2,1)S(1)}, bf16[1,27,64,64]{3,2,1,0:T(8,128)(2,1)}, u32[]{:S(2)}) copy-start(bf16[1,27,64,64]{3,2,1,0:T(8,128)(2,1)} %get-tuple-element.533) | copy-start | bytes 663556 | tf_op jit(solution)/shard_map/while
  141.8 6.8 %collective-permute-start = (bf16[64,1,64]{0,2,1:T(8,128)(2,1)S(1)}, bf16[64,1,64]{0,2,1:T(8,128)(2,1)S(1)}, u32[]{:S(2)}, u32[]{:S(2)}) collective-permute-start(bf16[64,1,64]{0,2,1:T(8,128)(2,1)S(1)} %get-tuple-element.480), channel_id=1, source_target_pairs={{1,0},{2,1},{3,2},{4,3},{5,4},{6,5},{7,6},{9,8},{10,9},{11,10},{12... | collective-permute-start | bytes 24584 | tf_op jit(solution)/shard_map/while/body/eval_jaxpr/ppermute | solution.py:22
  143.1 6.9 %collective-permute-start.1 = (bf16[64,1,64]{0,2,1:T(8,128)(2,1)S(1)}, bf16[64,1,64]{0,2,1:T(8,128)(2,1)S(1)}, u32[]{:S(2)}, u32[]{:S(2)}) collective-permute-start(bf16[64,1,64]{0,2,1:T(8,128)(2,1)S(1)} %get-tuple-element.481), channel_id=1, source_target_pairs={{0,1},{1,2},{2,3},{3,4},{4,5},{5,6},{6,7},{8,9},{9,10},{10,11},{11... | collective-permute-start | bytes 24584 | tf_op jit(solution)/shard_map/while/body/eval_jaxpr/ppermute | solution.py:19
  160.5 11.5 %copy-start.2 = (bf16[1,27,64,64]{3,2,1,0:T(8,128)(2,1)S(1)}, bf16[1,27,64,64]{3,2,1,0:T(8,128)(2,1)}, u32[]{:S(2)}) copy-start(bf16[1,27,64,64]{3,2,1,0:T(8,128)(2,1)} %get-tuple-element.535) | copy-start | bytes 663556 | tf_op jit(solution)/shard_map/while
  162.9 6.8 %collective-permute-start.2 = (bf16[64,1,256]{2,0,1:T(8,128)(2,1)S(1)}, bf16[64,1,256]{2,0,1:T(8,128)(2,1)S(1)}, u32[]{:S(2)}, u32[]{:S(2)}) collective-permute-start(bf16[64,1,256]{2,0,1:T(8,128)(2,1)S(1)} %get-tuple-element.483), channel_id=1, source_target_pairs={{1,0},{2,1},{3,2},{4,3},{5,4},{6,5},{7,6},{9,8},{10,9},{11,10},{12... | collective-permute-start | bytes 98312 | tf_op jit(solution)/shard_map/while/body/eval_jaxpr/ppermute | solution.py:22
  164.2 7.0 %collective-permute-start.3 = (bf16[64,1,256]{2,0,1:T(8,128)(2,1)S(1)}, bf16[64,1,256]{2,0,1:T(8,128)(2,1)S(1)}, u32[]{:S(2)}, u32[]{:S(2)}) collective-permute-start(bf16[64,1,256]{2,0,1:T(8,128)(2,1)S(1)} %get-tuple-element.484), channel_id=1, source_target_pairs={{0,1},{1,2},{2,3},{3,4},{4,5},{5,6},{6,7},{8,9},{9,10},{10,11},{11... | collective-permute-start | bytes 98312 | tf_op jit(solution)/shard_map/while/body/eval_jaxpr/ppermute | solution.py:19
  176.6 5.0 %collective-permute-start.4 = (bf16[64,4,256]{2,0,1:T(8,128)(2,1)S(1)}, bf16[64,4,256]{2,0,1:T(8,128)(2,1)S(1)}, u32[]{:S(2)}, u32[]{:S(2)}) collective-permute-start(bf16[64,4,256]{2,0,1:T(8,128)(2,1)S(1)} %get-tuple-element.497), channel_id=1, source_target_pairs={{8,0},{16,8},{24,16},{9,1},{17,9},{25,17},{10,2},{18,10},{26,18},{... | collective-permute-start | bytes 393224 | tf_op jit(solution)/shard_map/while/body/eval_jaxpr/ppermute | solution.py:30
  194.3 147.2 %all-gather.2.cloned.1.call-start = ((), (), s32[]{:S(2)}) async-start(), calls=%async_computation.1 | async-start | bytes 3981312 | tf_op jit(solution)/shard_map/all_gather | solution.py:194
Sparse Core Ops, SparseCore 0:
  194.5 80.5 all-reduce.5
  277.8 63.6 all-gather.1
